TPU v7x, 32 devices: a whole 2x2x4 slice. The times are simulated.
32 devices in a mesh: col: 16 (over z, y, x), grp: 2 (over core).
Axes of the slice: x: 2, y: 2, z: 4, core: 2. Of those that a mesh axis runs over, the one named last changes fastest.
Arguments:
- diag_blocks: float32 [16, 128, 128], P('col'), as said below
- panel_blocks: float32 [16, 2, 128, 128], P('col', 'grp'), as said below
- targets: int32 [16, 2], replicated, may hold values from 0 to 16, as said below
Outputs:
- factor_diag: float32 [16, 128, 128], P('col')
- factor_panel: float32 [16, 2, 128, 128], P('col', 'grp')
Inputs may be any that keep to these rules, and one draw needn't show every extreme that they name: targets[s, 0] is the parent of supernode s and targets[s, 1] = targets[targets[s, 0], 0] its grandparent, 16 where that ancestor lies outside the window; the tree is a binary heap under a random labelling: exactly one root, every supernode has at most two children and at most four grandchildren, and level d holds min(2 ** d, 16 - 2 ** d + 1) supernodes. `diag_blocks`: each block is symmetric positive definite, and every updated diagonal block stays positive definite. `panel_blocks`: every entry lies within 8 / sqrt(128) of zero.
All inputs are finite; a program needn't handle non-finite values.
Results may differ from a plain program's by a relative error of at most 0.00095.
Values may be sent and summed in bfloat16 or wider, within the bound.
A program may use at most 64 MiB of HBM per device.

v0:
```python
import jax
import jax.numpy as jnp
from jax import lax
from jax.sharding import PartitionSpec as P


def spread(x, axis, root):
    mine = lax.axis_index(axis) == root
    return lax.psum(jnp.where(mine, x, jnp.zeros_like(x)), axis)


def from_partner(x, axis, apart):
    return lax.ppermute(x, axis, [(i, i ^ 1 << apart) for i in range(lax.axis_size(axis))])


def node_depth(parent, nodes):
    extended = jnp.concatenate([parent, jnp.array([nodes], jnp.int32)])
    depth = jnp.zeros((nodes,), jnp.int32)
    current = parent
    for index in range(nodes.bit_length()):
        depth = depth + (current < nodes).astype(jnp.int32)
        current = extended[current]
    return depth


def solve_right(lower, panel):

    def one(factor, block):
        return jax.scipy.linalg.solve_triangular(factor, block.T, lower=True).T

    return jax.vmap(one)(lower, panel)


def sibling_rank(target, nodes):
    earlier = jnp.arange(nodes)[None, :] < jnp.arange(nodes)[:, None]
    same = target[:, None] == target[None, :]
    return jnp.sum((same & earlier).astype(jnp.int32), axis=1)


def slot_picker(target, rank, active_nodes, owned_ids, count):
    match = target[None, None, :] == owned_ids[:, None, None]
    match = match & (rank[None, None, :] == jnp.arange(count)[None, :, None])
    match = match & active_nodes[None, None, :]
    return match.astype(jnp.bfloat16)


def select_rows(picker, block_list):
    return jnp.einsum("iqc,cab->iqab", picker, block_list, preferred_element_type=jnp.float32)


def outer_sum(block_list):
    return jnp.einsum("hync,hyxc->hnx", block_list, block_list, preferred_element_type=jnp.float32)


def cross_sum(left_factor, right_factor):
    return jnp.einsum(
        "hync,hyxc->hnx", left_factor, right_factor, preferred_element_type=jnp.float32
    )


def pair_cores(sent):
    return lax.all_gather(sent[:, None], "grp", axis=1, tiled=True)


def spread_nodes(sent, active_nodes, pick_near, pick_far, slots, nodes, present, blanks):
    paired = pair_cores(sent)
    order = jnp.argsort(jnp.where(active_nodes, 0, 1) * nodes + jnp.arange(nodes, dtype=jnp.int32))

    def visit(index, carry):
        node = order[index]
        piece = lax.dynamic_index_in_dim(paired, node % slots, 0, keepdims=False)
        arrived = spread(piece, "col", node // slots).astype(jnp.float32)
        weight_near = lax.dynamic_index_in_dim(pick_near, node, 2, keepdims=False).astype(
            jnp.float32
        )
        weight_far = lax.dynamic_index_in_dim(pick_far, node, 2, keepdims=False).astype(jnp.float32)
        return (
            carry[0] + weight_near[:, :, None, None] * arrived[0][None, None],
            carry[1] + weight_far[:, :, None, None] * arrived[1][None, None],
            carry[2] + weight_near[:, :, None, None] * arrived[1][None, None],
        )

    return lax.fori_loop(0, present, visit, blanks)


def shards(diag_blocks, panel_blocks, targets):
    slots = diag_blocks.shape[0]
    width = diag_blocks.shape[1]
    nodes = targets.shape[0]
    core = lax.axis_index("grp")
    owned_ids = lax.axis_index("col") * slots + jnp.arange(slots, dtype=jnp.int32)
    parent = targets[:, 0]
    grand = targets[:, 1]
    depth = node_depth(parent, nodes)
    rank_near = sibling_rank(parent, nodes)
    rank_far = sibling_rank(grand, nodes)
    owned_tree_depth = jnp.take(depth, owned_ids)
    acc_diag = diag_blocks
    acc_panel = panel_blocks[:, 0]
    out_diag = jnp.zeros_like(diag_blocks)
    output_panel = jnp.zeros_like(acc_panel)
    empty_pair_slots = jnp.zeros((slots, 2, width, width), jnp.float32)
    blank_four = jnp.zeros((slots, 4, width, width), jnp.float32)
    for level in range(nodes.bit_length() - 1, -1, -1):
        wide_mask = (owned_tree_depth == level)[:, None, None]
        lower = jnp.linalg.cholesky(acc_diag)
        solved = solve_right(lower, acc_panel)
        out_diag = jnp.where(wide_mask, lower, out_diag)
        output_panel = jnp.where(wide_mask, solved, output_panel)
        if level == 0:
            break
        sent = jnp.where(wide_mask, solved, 0.0).astype(jnp.bfloat16)
        active_nodes = depth == level
        pick_near = slot_picker(parent, rank_near, active_nodes, owned_ids, 2)
        pick_far = slot_picker(grand, rank_far, active_nodes, owned_ids, 4)
        present = min(2**level, nodes - 2**level + 1)
        crowded = present * 4 > nodes
        if crowded:
            piece = lax.all_gather(sent, "col", axis=0, tiled=True)
            near_rows = select_rows(pick_near, piece)
            far_rows = select_rows(pick_far, piece)
            near_rows = near_rows.astype(jnp.bfloat16)
            far_rows = far_rows.astype(jnp.bfloat16)
            own_update = lax.cond(
                core == 0, lambda: outer_sum(near_rows), lambda: outer_sum(far_rows)
            )
            other_update, other_rows = (
                from_partner(own_update.astype(jnp.bfloat16), "grp", 0).astype(own_update.dtype),
                from_partner(near_rows, "grp", 0),
            )
            schur_update = own_update + other_update
            cross = cross_sum(other_rows, near_rows)
        else:
            kids, grandkids, kids_far = spread_nodes(
                sent,
                active_nodes,
                pick_near,
                pick_far,
                slots,
                nodes,
                present,
                (empty_pair_slots, blank_four, empty_pair_slots),
            )
            kids = kids.astype(jnp.bfloat16)
            schur_update = outer_sum(kids) + outer_sum(grandkids.astype(jnp.bfloat16))
            cross = cross_sum(kids_far.astype(jnp.bfloat16), kids)
        acc_diag = acc_diag - schur_update
        acc_panel = acc_panel - jnp.where(core == 0, cross, 0.0)
    return (out_diag, output_panel[:, None])


def solution(mesh):
    placed = (P("col", None, None), P("col", "grp", None, None), P())
    return jax.shard_map(
        shards,
        mesh=mesh,
        in_specs=placed,
        out_specs=(P("col", None, None), P("col", "grp", None, None)),
        check_vma=False,
    )
```

profile of v0, /device:TPU:1, one launch (start us, length us, event | category | flops | bytes accessed | tf_op | source)
XLA Modules:
  0.0 959.5 jit_solution(17685611445959303273)
XLA Ops:
  7.2 0.6 copy-done.2
  7.9 0.7 gather_fusion
  8.6 0.7 gather_fusion.1
  9.3 0.7 gather_fusion.2
  10.0 0.7 gather_fusion.3
  10.7 0.7 dynamic-slice.2
  11.5 11.7 %custom-call.20 = f32[1,128,128]{2,1,0:T(8,128)S(1)} custom-call(f32[1,128,128]{2,1,0:T(8,128)S(1)} %fusion.50), custom_call_target="Cholesky" | custom-call | tf_op jit(solution)/shard_map/jit(cholesky)/cholesky | solution.py:106
  23.2 0.7 compare_reduce_fusion.4
  23.9 0.7 fusion.69
  24.5 9.8 %custom-call.21 = f32[1,1,128,128]{2,3,1,0:T(8,128)S(1)} custom-call(f32[1,1,128,128]{3,2,1,0:T(8,128)S(1)} %fusion.69), custom_call_target="InvertDiagBlocksLowerTriangular" | custom-call | tf_op jit(solution)/shard_map/vmap(jit(_solve_triangular))/triangular_solve | solution.py:29
  35.5 2.0 all-gather
  37.5 1.2 sort.45
  38.8 0.6 broadcast_select_fusion
  40.5 0.7 fusion.114
  41.2 0.7 fusion.112
  41.9 101.4 %all-reduce.4.cloned.1.call-done = bf16[2,128,128]{2,1,0:T(8,128)(2,1)} async-done(((bf16[2,128,128]{2,1,0:T(8,128)(2,1)}), bf16[2,128,128]{2,1,0:T(8,128)(2,1)}) %all-reduce.4.cloned.1.call-update) | async-done | bytes 65552 | tf_op jit(solution)/shard_map/while/body/eval_jaxpr/psum | solution.py:9
  143.3 0.8 convert_element_type.377
  145.0 11.7 %custom-call.22 = f32[1,128,128]{2,1,0:T(8,128)S(1)} custom-call(f32[1,128,128]{2,1,0:T(8,128)S(1)} %fusion.48), custom_call_target="Cholesky" | custom-call | tf_op jit(solution)/shard_map/jit(cholesky)/cholesky | solution.py:106
  156.8 0.7 compare_reduce_fusion.3
  157.5 0.6 fusion.70
  158.1 9.8 %custom-call.23 = f32[1,1,128,128]{2,3,1,0:T(8,128)S(1)} custom-call(f32[1,1,128,128]{3,2,1,0:T(8,128)S(1)} %fusion.70), custom_call_target="InvertDiagBlocksLowerTriangular" | custom-call | tf_op jit(solution)/shard_map/vmap(jit(_solve_triangular))/triangular_solve | solution.py:29
  168.4 34.6 %all_gather.13 = bf16[16,128,128]{2,1,0:T(8,128)(2,1)S(1)} all-gather(bf16[1,128,128]{2,1,0:T(8,128)(2,1)S(1)} %copy.89), channel_id=1, replica_groups=mesh['col'=16,'grp'=2] {'col'}, dimensions={0}, use_global_device_ids=true | all-gather | bytes 557056 | tf_op jit(solution)/shard_map/all_gather | solution.py:119
  204.2 9.7 %collective-permute-start = (bf16[1,128,128]{1,2,0:T(8,128)(2,1)S(1)}, bf16[1,128,128]{1,2,0:T(8,128)(2,1)S(1)}, u32[]{:S(2)}, u32[]{:S(2)}) collective-permute-start(bf16[1,128,128]{1,2,0:T(8,128)(2,1)S(1)} %convert_bitcast_fusion), channel_id=1, source_target_pairs={{0,1},{1,0},{2,3},{3,2},{4,5},{5,4},{6,7},{7,6},{8,9},{9,8},{10,11... | collective-permute-start | bytes 98312 | tf_op jit(solution)/shard_map/ppermute | solution.py:13
  214.0 1.2 sort.46
  215.2 1.2 sort.47
  216.7 11.7 %custom-call.24 = f32[1,128,128]{2,1,0:T(8,128)S(1)} custom-call(f32[1,128,128]{2,1,0:T(8,128)S(1)} %fusion.45), custom_call_target="Cholesky" | custom-call | tf_op jit(solution)/shard_map/jit(cholesky)/cholesky | solution.py:106
  228.4 0.7 compare_reduce_fusion.2
  229.1 0.6 fusion.71
  229.7 9.8 %custom-call.25 = f32[1,1,128,128]{2,3,1,0:T(8,128)S(1)} custom-call(f32[1,1,128,128]{3,2,1,0:T(8,128)S(1)} %fusion.71), custom_call_target="InvertDiagBlocksLowerTriangular" | custom-call | tf_op jit(solution)/shard_map/vmap(jit(_solve_triangular))/triangular_solve | solution.py:29
  240.2 2.2 all-gather.1
  242.4 435.9 %while.48 = (s32[]{:T(128)}, f32[1,2,128,128]{3,2,1,0:T(8,128)S(1)}, f32[1,4,128,128]{3,2,1,0:T(8,128)S(1)}, f32[1,2,128,128]{3,2,1,0:T(8,128)S(1)}, s32[16]{0:T...) while((s32[]{:T(128)}, ...), condition=%wide.region_11.14_spmd.clone, body=%wide.region_9.13_spmd.clone.sunk | while | flops 491536 | bytes 2228556 | solution.py:83
  242.4 0.6 dynamic_slice.120
  243.6 0.6 select_bitcast_fusion.5
  246.2 100.2 %all-reduce.6.cloned.1.call-done = bf16[2,128,128]{2,1,0:T(8,128)(2,1)} async-done(((bf16[2,128,128]{2,1,0:T(8,128)(2,1)}), bf16[2,128,128]{2,1,0:T(8,128)(2,1)}) %all-reduce.6.cloned.1.call-update) | async-done | bytes 65552 | tf_op jit(solution)/shard_map/while/body/eval_jaxpr/psum | solution.py:9
  346.4 0.8 convert_element_type.518
  347.6 0.7 dynamic_slice.120
  348.8 0.6 select_bitcast_fusion.5
  351.4 105.5 %all-reduce.6.cloned.1.call-done = bf16[2,128,128]{2,1,0:T(8,128)(2,1)} async-done(((bf16[2,128,128]{2,1,0:T(8,128)(2,1)}), bf16[2,128,128]{2,1,0:T(8,128)(2,1)}) %all-reduce.6.cloned.1.call-update) | async-done | bytes 65552 | tf_op jit(solution)/shard_map/while/body/eval_jaxpr/psum | solution.py:9
  456.9 0.8 convert_element_type.518
  458.0 0.7 dynamic_slice.120
  459.3 0.6 select_bitcast_fusion.5
  461.9 105.2 %all-reduce.6.cloned.1.call-done = bf16[2,128,128]{2,1,0:T(8,128)(2,1)} async-done(((bf16[2,128,128]{2,1,0:T(8,128)(2,1)}), bf16[2,128,128]{2,1,0:T(8,128)(2,1)}) %all-reduce.6.cloned.1.call-update) | async-done | bytes 65552 | tf_op jit(solution)/shard_map/while/body/eval_jaxpr/psum | solution.py:9
  567.0 0.8 convert_element_type.518
  568.2 0.7 dynamic_slice.120
  569.4 0.6 select_bitcast_fusion.5
  572.0 105.2 %all-reduce.6.cloned.1.call-done = bf16[2,128,128]{2,1,0:T(8,128)(2,1)} async-done(((bf16[2,128,128]{2,1,0:T(8,128)(2,1)}), bf16[2,128,128]{2,1,0:T(8,128)(2,1)}) %all-reduce.6.cloned.1.call-update) | async-done | bytes 65552 | tf_op jit(solution)/shard_map/while/body/eval_jaxpr/psum | solution.py:9
  677.2 0.8 convert_element_type.518
  678.7 11.7 %custom-call.26 = f32[1,128,128]{2,1,0:T(8,128)S(1)} custom-call(f32[1,128,128]{2,1,0:T(8,128)S(1)} %fusion.41), custom_call_target="Cholesky" | custom-call | tf_op jit(solution)/shard_map/jit(cholesky)/cholesky | solution.py:106
  690.5 0.7 compare_reduce_fusion.1
  691.2 0.6 fusion.72
  691.8 9.8 %custom-call.27 = f32[1,1,128,128]{2,3,1,0:T(8,128)S(1)} custom-call(f32[1,1,128,128]{3,2,1,0:T(8,128)S(1)} %fusion.72), custom_call_target="InvertDiagBlocksLowerTriangular" | custom-call | tf_op jit(solution)/shard_map/vmap(jit(_solve_triangular))/triangular_solve | solution.py:29
  702.2 4.4 all-gather.2
  706.6 218.4 %while.49 = (s32[]{:T(128)}, f32[1,2,128,128]{3,2,1,0:T(8,128)S(1)}, f32[1,4,128,128]{3,2,1,0:T(8,128)S(1)}, f32[1,2,128,128]{3,2,1,0:T(8,128)S(1)}, s32[16]{0:T...) while((s32[]{:T(128)}, ...), condition=%wide.region_15.18_spmd.clone, body=%wide.region_13.17_spmd.clone.sunk | while | flops 491536 | bytes 2228556 | solution.py:83
  707.8 0.6 select_bitcast_fusion.6
  710.5 103.0 %all-reduce.8.cloned.1.call-done = bf16[2,128,128]{2,1,0:T(8,128)(2,1)} async-done(((bf16[2,128,128]{2,1,0:T(8,128)(2,1)}), bf16[2,128,128]{2,1,0:T(8,128)(2,1)}) %all-reduce.8.cloned.1.call-update) | async-done | bytes 65552 | tf_op jit(solution)/shard_map/while/body/eval_jaxpr/psum | solution.py:9
  813.4 0.8 convert_element_type.519
  815.8 0.6 select_bitcast_fusion.6
  818.5 105.4 %all-reduce.8.cloned.1.call-done = bf16[2,128,128]{2,1,0:T(8,128)(2,1)} async-done(((bf16[2,128,128]{2,1,0:T(8,128)(2,1)}), bf16[2,128,128]{2,1,0:T(8,128)(2,1)}) %all-reduce.8.cloned.1.call-update) | async-done | bytes 65552 | tf_op jit(solution)/shard_map/while/body/eval_jaxpr/psum | solution.py:9
  923.9 0.8 convert_element_type.519
  925.5 11.7 %custom-call.28 = f32[1,128,128]{2,1,0:T(8,128)S(1)} custom-call(f32[1,128,128]{2,1,0:T(8,128)S(1)} %fusion.36), custom_call_target="Cholesky" | custom-call | tf_op jit(solution)/shard_map/jit(cholesky)/cholesky | solution.py:106
  937.2 0.6 compare_reduce_fusion
  937.9 3.8 select_bitcast_fusion.2
  941.7 9.8 %custom-call.29 = f32[1,1,128,128]{2,3,1,0:T(8,128)S(1)} custom-call(f32[1,1,128,128]{3,2,1,0:T(8,128)S(1)} %get-tuple-element.605), custom_call_target="InvertDiagBlocksLowerTriangular" | custom-call | tf_op jit(solution)/shard_map/vmap(jit(_solve_triangular))/triangular_solve | solution.py:29
  951.9 0.7 copy.107
  (124 shorter events, 10.0 us)
Async XLA Ops:
  7.2 0.7 copy-start.2
  7.2 136.1 %all-reduce.4.cloned.1.call-start = ((), (), s32[]{:S(2)}) async-start(), calls=%async_computation | async-start | bytes 131072 | tf_op jit(solution)/shard_map/while/body/eval_jaxpr/psum | solution.py:9
  10.0 1.4 copy-start
  23.9 11.2 %copy-start.1 = (f32[1,1,128,128]{3,2,1,0:T(8,128)S(1)}, f32[1,1,128,128]{3,2,1,0:T(8,128)}, u32[]{:S(2)}) copy-start(f32[1,1,128,128]{3,2,1,0:T(8,128)} %param.14) | copy-start | bytes 196612
  204.2 12.3 %collective-permute-start = (bf16[1,128,128]{1,2,0:T(8,128)(2,1)S(1)}, bf16[1,128,128]{1,2,0:T(8,128)(2,1)S(1)}, u32[]{:S(2)}, u32[]{:S(2)}) collective-permute-start(bf16[1,128,128]{1,2,0:T(8,128)(2,1)S(1)} %convert_bitcast_fusion), channel_id=1, source_target_pairs={{0,1},{1,0},{2,3},{3,2},{4,5},{5,4},{6,7},{7,6},{8,9},{9,8},{10,11... | collective-permute-start | bytes 98312 | tf_op jit(solution)/shard_map/ppermute | solution.py:13
  216.5 23.1 %collective-permute-start.1 = (bf16[1,2,128,128]{3,1,2,0:T(2,128)(2,1)S(1)}, bf16[1,2,128,128]{3,1,2,0:T(2,128)(2,1)S(1)}, u32[]{:S(2)}, u32[]{:S(2)}) collective-permute-start(bf16[1,2,128,128]{3,1,2,0:T(2,128)(2,1)S(1)} %bitcast.322), channel_id=1, source_target_pairs={{0,1},{1,0},{2,3},{3,2},{4,5},{5,4},{6,7},{7,6},{8,9},{9,8},{10,11... | collective-permute-start | bytes 196616 | tf_op jit(solution)/shard_map/ppermute | solution.py:13
  242.4 104.1 %all-reduce.6.cloned.1.call-start = ((), (), s32[]{:S(2)}) async-start(), calls=%async_computation.1 | async-start | bytes 131072 | tf_op jit(solution)/shard_map/while/body/eval_jaxpr/psum | solution.py:9
  347.5 109.4 %all-reduce.6.cloned.1.call-start = ((), (), s32[]{:S(2)}) async-start(), calls=%async_computation.1 | async-start | bytes 131072 | tf_op jit(solution)/shard_map/while/body/eval_jaxpr/psum | solution.py:9
  458.0 109.1 %all-reduce.6.cloned.1.call-start = ((), (), s32[]{:S(2)}) async-start(), calls=%async_computation.1 | async-start | bytes 131072 | tf_op jit(solution)/shard_map/while/body/eval_jaxpr/psum | solution.py:9
  568.1 109.1 %all-reduce.6.cloned.1.call-start = ((), (), s32[]{:S(2)}) async-start(), calls=%async_computation.1 | async-start | bytes 131072 | tf_op jit(solution)/shard_map/while/body/eval_jaxpr/psum | solution.py:9
  706.6 106.8 %all-reduce.8.cloned.1.call-start = ((), (), s32[]{:S(2)}) async-start(), calls=%async_computation.2 | async-start | bytes 131072 | tf_op jit(solution)/shard_map/while/body/eval_jaxpr/psum | solution.py:9
  814.5 109.4 %all-reduce.8.cloned.1.call-start = ((), (), s32[]{:S(2)}) async-start(), calls=%async_computation.2 | async-start | bytes 131072 | tf_op jit(solution)/shard_map/while/body/eval_jaxpr/psum | solution.py:9
Sparse Core Ops, SparseCore 0:
  39.6 103.6 all-reduce.3
  249.2 97.1 all-reduce.5
  354.4 102.4 all-reduce.5
  464.5 102.4 all-reduce.5
  574.7 102.4 all-reduce.5
  713.1 100.2 all-reduce.7
  821.4 102.4 all-reduce.7
where the time goes:
time: 963 us; the launch traced here: 960 us
  waiting for transfers between devices  726 us (75%)
  other arithmetic  135 us (14%)
  blocking collectives  43.2 us (4%)
  loops' own time  15.8 us (2%)
  between operations  15.4 us (2%)
  local copies, waits for them, and re-layouts  10 us (1%)
  starting transfers between devices  10 us (1%)
    psum x7, waiting for transfers between devices, spread(): return lax.psum(jnp.where(mine, x, jnp.zeros_like(x)), axis)  726 us
    another operation x15, other arithmetic, shards(): lower = jnp.linalg.cholesky(acc_diag)  62.1 us
    another operation x10, other arithmetic, one(): return jax.scipy.linalg.solve_triangular(factor, block.T, lower=True).T  55.4 us
    all_gather x1, blocking collectives, shards(): piece = lax.all_gather(sent, 'col', axis=0, tiled=True)  34.6 us
  transfers between devices with their start and end apart: 9, of which 7 were waited for; matrix products, arithmetic and copies ran while one was open for 3% of the time, Pallas kernels for 0%

commit v1 on v0

v1 whole, which is shorter than its diff:
```python
import functools

import jax
import jax.numpy as jnp
from jax import lax
from jax.experimental import pallas as pl
from jax.experimental.pallas import tpu as pltpu
from jax.sharding import PartitionSpec as P

MESH = pl.DeviceIdType.MESH
BLOCK = 16
HIGHEST = lax.Precision.HIGHEST


def across(value, width):
    return jnp.broadcast_to(value, (value.shape[0], width))


def factor_rows(work, width):
    total = 2 * width
    for first in range(0, width, BLOCK):
        rows = work[first:first + BLOCK, :]
        columns = [across(rows[:, first + j:first + j + 1], 128) for j in range(BLOCK)]
        index = lax.broadcasted_iota(jnp.int32, (BLOCK, 128), 0)
        done = []
        for j in range(BLOCK):
            pivot = columns[j][j:j + 1, :]
            inverse = lax.rsqrt(pivot)
            scaled = columns[j] * inverse
            below = jnp.where(index > j, scaled, 0.0)
            for k in range(j + 1, BLOCK):
                entry = scaled[k:k + 1, :]
                columns[k] = columns[k] - below * entry
            lead = [rows[j:j + 1, h:h + 128] * inverse for h in range(0, total, 128)]
            lead = jnp.concatenate(lead, 1)
            done.append(lead)
            if j + 1 < BLOCK:
                wide = jnp.concatenate([below] * (total // 128), 1)
                rows = rows - wide * lead
        upper = jnp.concatenate(done, 0)
        work[first:first + BLOCK, :] = upper
        if first + BLOCK < width:
            left = upper[:, :width]
            change = lax.dot_general(left, upper, (((0,), (0,)), ((), ())),
                                     precision=HIGHEST, preferred_element_type=jnp.float32)
            work[first + BLOCK:, :] = work[first + BLOCK:, :] - change[first + BLOCK:, :]


def kernel(nodes, levels, targets, diag, panel, out_diag, out_panel, acc, work, part,
           got_part, kids_out, kids_in, send_sem, recv_sem, pair_send, pair_recv, *slots):
    width = diag.shape[-1]
    me = lax.axis_index("col")
    core = lax.axis_index("grp")

    barrier = pltpu.get_barrier_semaphore()

    def greet(offset, carry):
        peer = lax.rem(me + offset, nodes)
        pl.semaphore_signal(barrier, inc=1, device_id=(peer, core), device_id_type=MESH)
        return carry

    lax.fori_loop(1, nodes, greet, 0)
    pl.semaphore_signal(barrier, inc=1, device_id=(me, 1 - core), device_id_type=MESH)

    acc[:, :width] = diag[...]
    acc[:, width:] = panel[...].T

    def parent_of(node):
        return jnp.where(node < nodes, targets[jnp.minimum(node, nodes - 1), 0], nodes)

    depth = jnp.int32(0)
    current = targets[me, 0]
    for _ in range(levels - 1):
        depth = depth + (current < nodes).astype(jnp.int32)
        current = parent_of(current)

    def search(node, carry):
        kid = targets[node, 0] == me
        grand = targets[node, 1] == me
        k0, k1, kc, g0, g1, g2, g3, gc = carry
        k0 = jnp.where(kid & (kc == 0), node, k0)
        k1 = jnp.where(kid & (kc == 1), node, k1)
        kc = kc + kid.astype(jnp.int32)
        g0 = jnp.where(grand & (gc == 0), node, g0)
        g1 = jnp.where(grand & (gc == 1), node, g1)
        g2 = jnp.where(grand & (gc == 2), node, g2)
        g3 = jnp.where(grand & (gc == 3), node, g3)
        gc = gc + grand.astype(jnp.int32)
        return k0, k1, kc, g0, g1, g2, g3, gc

    zero = jnp.int32(0)
    k0, k1, kc, g0, g1, g2, g3, gc = lax.fori_loop(0, nodes, search, (zero,) * 8)
    near_core = core == 0
    picks = [jnp.where(near_core, k0, g0), jnp.where(near_core, k1, g1), g2, g3]
    own_count = jnp.where(near_core, kc, gc)
    own_apart = jnp.where(near_core, 1, 2)

    pl.semaphore_wait(barrier, nodes)

    def pick(held, node, wanted):
        rows = held[node]
        return jnp.where(wanted, rows, jnp.zeros_like(rows))

    def send(step, held, solved):
        held[me] = solved.astype(jnp.bfloat16)

        def start(offset, carry):
            peer = lax.rem(me + offset, nodes)
            pltpu.make_async_remote_copy(
                src_ref=held.at[me], dst_ref=held.at[me],
                send_sem=send_sem.at[step], recv_sem=recv_sem.at[step],
                device_id=(peer, core), device_id_type=MESH).start()
            return carry

        lax.fori_loop(1, nodes, start, 0)

    def gather(step, held):
        level = levels - 1 - step
        everyone = held.at[pl.ds(0, nodes - 1)]
        pltpu.make_async_copy(everyone, everyone, recv_sem.at[step]).wait()
        is_kid = depth + 1 == level
        kid_a = pick(held, k0, is_kid & (kc > 0))
        kid_b = pick(held, k1, is_kid & (kc > 1))
        kids_out[step, :, :width] = kid_a
        kids_out[step, :, width:] = kid_b
        rows_copy = pltpu.make_async_remote_copy(
            src_ref=kids_out.at[step], dst_ref=kids_in.at[step],
            send_sem=pair_send.at[step, 0], recv_sem=pair_recv.at[step, 0],
            device_id=(me, 1 - core), device_id_type=MESH)
        rows_copy.start()
        mine = depth + own_apart == level
        four = [pick(held, picks[0], mine & (own_count > 0)),
                pick(held, picks[1], mine & (own_count > 1)),
                pick(held, picks[2], mine & (own_count > 2)),
                pick(held, picks[3], mine & (own_count > 3))]
        four = jnp.concatenate(four, 1)
        own = lax.dot_general(four, four, (((1,), (1,)), ((), ())),
                              preferred_element_type=jnp.float32)
        part[step] = own
        part_copy = pltpu.make_async_remote_copy(
            src_ref=part.at[step], dst_ref=got_part.at[step],
            send_sem=pair_send.at[step, 1], recv_sem=pair_recv.at[step, 1],
            device_id=(me, 1 - core), device_id_type=MESH)
        part_copy.start()
        rows_copy.wait()
        kids = jnp.concatenate([kid_a, kid_b], 1)
        cross = lax.dot_general(kids, kids_in[step], (((1,), (1,)), ((), ())),
                                preferred_element_type=jnp.float32)
        acc[:, width:] = acc[:, width:] - jnp.where(near_core, cross, 0.0)
        part_copy.wait()
        acc[:, :width] = acc[:, :width] - (own + got_part[step])
        pltpu.make_async_copy(everyone, everyone, send_sem.at[step]).wait()

    def level_step(step, carry):
        level = levels - 1 - step
        work[...] = acc[...]
        factor_rows(work, width)
        solved = work[:, width:].T
        active = depth == level

        for turn in range(levels - 1):
            pl.when(step == turn)(functools.partial(send, turn, slots[turn], solved))

        tri = lax.broadcasted_iota(jnp.int32, (width, width), 0)
        tri = tri >= lax.broadcasted_iota(jnp.int32, (width, width), 1)
        lower = jnp.where(tri, work[:, :width].T, 0.0)
        out_diag[...] = jnp.where(active, lower, out_diag[...])
        out_panel[...] = jnp.where(active, solved, out_panel[...])

        for turn in range(levels - 1):
            pl.when(step == turn)(functools.partial(gather, turn, slots[turn]))

        return carry

    out_diag[...] = jnp.zeros_like(out_diag)
    out_panel[...] = jnp.zeros_like(out_panel)
    lax.fori_loop(0, levels, level_step, 0)


def shards(diag_blocks, panel_blocks, targets):
    width = diag_blocks.shape[1]
    nodes = targets.shape[0]
    levels = nodes.bit_length()
    steps = levels - 1
    vmem = pl.BlockSpec(memory_space=pltpu.VMEM)
    dma = pltpu.SemaphoreType.DMA
    square = jax.ShapeDtypeStruct((width, width), jnp.float32)
    lower, solved = pl.pallas_call(
        functools.partial(kernel, nodes, levels),
        out_shape=(square, square),
        in_specs=[pl.BlockSpec(memory_space=pltpu.SMEM), vmem, vmem],
        out_specs=(vmem, vmem),
        scratch_shapes=[
            pltpu.VMEM((width, 2 * width), jnp.float32),
            pltpu.VMEM((width, 2 * width), jnp.float32),
            pltpu.VMEM((steps, width, width), jnp.float32),
            pltpu.VMEM((steps, width, width), jnp.float32),
            pltpu.VMEM((steps, width, 2 * width), jnp.bfloat16),
            pltpu.VMEM((steps, width, 2 * width), jnp.bfloat16),
            dma((steps,)), dma((steps,)), dma((steps, 2)), dma((steps, 2)),
        ] + [pltpu.VMEM((nodes, width, width), jnp.bfloat16)] * steps,
        compiler_params=pltpu.CompilerParams(collective_id=0, has_side_effects=True),
    )(targets, diag_blocks.reshape(width, width), panel_blocks.reshape(width, width))
    return lower[None], solved[None, None]


def solution(mesh):
    return jax.shard_map(
        shards,
        mesh=mesh,
        in_specs=(P("col", None, None), P("col", "grp", None, None), P()),
        out_specs=(P("col", None, None), P("col", "grp", None, None)),
        check_vma=False,
    )
```

time: 963 us -> 90 us (0.09)
  the two profiles are of different devices: /device:TPU:1 before, /device:TPU:13 now
where the time goes in v1:
time: 90 us; the launch traced here: 89.8 us
  Pallas kernels  85.7 us (95%)
  local copies, waits for them, and re-layouts  3.49 us (4%)
    pallas_call x1, Pallas kernels, shards(): pl.pallas_call(functools.partial(kernel, nodes, levels), out_shape=(squar...  85.7 us
    unnamed x7, local copies, waits for them, and re-layouts  3.49 us

profile of v1, /device:TPU:13, one launch (start us, length us, event | category | flops | bytes accessed | tf_op | source)
XLA Modules:
  0.0 89.8 jit_solution(1839072367672347261)
XLA Ops:
  0.6 0.0 copy-start.1
  0.6 0.7 copy-done.1
  1.3 0.7 copy.5.targets
  2.0 85.7 %shard_map.50 = (f32[128,128]{1,0:T(8,128)}, f32[128,128]{1,0:T(8,128)}) custom-call(s32[16,2]{1,0:T(8,128)} %copy.5.targets, f32[128,128]{1,0:T(8,128)} %bitcast.4, f32[128,128]{1,0:T(8,128)} %bitcast.5), custom_call_target="tpu_custom_call" | custom-call | tf_op jit(solution)/shard_map/pallas_call | solution.py:188
  87.7 0.0 copy-start
  87.7 1.5 %copy.8 = f32[1,128,128]{2,1,0:T(8,128)} copy(f32[1,128,128]{2,1,0:T(8,128)} %bitcast.7) | data formatting | bytes 131072
  89.2 0.0 copy-done
  89.2 0.6 copy.9
Async XLA Ops:
  0.6 0.7 copy-start.1
  87.7 1.5 %copy-start = (f32[128,128]{1,0:T(8,128)S(1)}, f32[128,128]{1,0:T(8,128)}, u32[]{:S(2)}) copy-start(f32[128,128]{1,0:T(8,128)} %get-tuple-element.5) | copy-start | bytes 196612

commit v2 on v1

--- a/solution.py
+++ b/solution.py
@@ -46,20 +46,26 @@
             work[first + BLOCK:, :] = work[first + BLOCK:, :] - change[first + BLOCK:, :]
 
 
-def kernel(nodes, levels, targets, diag, panel, out_diag, out_panel, acc, work, part,
-           got_part, kids_out, kids_in, send_sem, recv_sem, pair_send, pair_recv, *slots):
+def kernel(nodes, levels, inner, targets, diag, panel, out_diag, out_panel, acc, work, depths, part,
+           got_part, kids_out, kids_in, line_send, line_recv, plane_send, plane_recv, pair_send,
+           pair_recv, *slots):
     width = diag.shape[-1]
+    lines = nodes // inner
     me = lax.axis_index("col")
     core = lax.axis_index("grp")
+    my_line = lax.div(me, inner)
+    my_spot = lax.rem(me, inner)
+
+    def along(offset):
+        return lax.rem(my_line + offset, lines) * inner + my_spot
+
+    def within(offset):
+        return my_line * inner + lax.rem(my_spot + offset, inner)
 
     barrier = pltpu.get_barrier_semaphore()
-
-    def greet(offset, carry):
-        peer = lax.rem(me + offset, nodes)
+    peers = [along(o) for o in range(1, lines)] + [within(o) for o in range(1, inner)]
+    for peer in peers:
         pl.semaphore_signal(barrier, inc=1, device_id=(peer, core), device_id_type=MESH)
-        return carry
-
-    lax.fori_loop(1, nodes, greet, 0)
     pl.semaphore_signal(barrier, inc=1, device_id=(me, 1 - core), device_id_type=MESH)
 
     acc[:, :width] = diag[...]
@@ -68,15 +74,15 @@
     def parent_of(node):
         return jnp.where(node < nodes, targets[jnp.minimum(node, nodes - 1), 0], nodes)
 
-    depth = jnp.int32(0)
-    current = targets[me, 0]
-    for _ in range(levels - 1):
-        depth = depth + (current < nodes).astype(jnp.int32)
-        current = parent_of(current)
-
     def search(node, carry):
-        kid = targets[node, 0] == me
+        current = targets[node, 0]
+        kid = current == me
         grand = targets[node, 1] == me
+        level = jnp.int32(0)
+        for _ in range(levels - 1):
+            level = level + (current < nodes).astype(jnp.int32)
+            current = parent_of(current)
+        depths[node] = level
         k0, k1, kc, g0, g1, g2, g3, gc = carry
         k0 = jnp.where(kid & (kc == 0), node, k0)
         k1 = jnp.where(kid & (kc == 1), node, k1)
@@ -90,37 +96,78 @@
 
     zero = jnp.int32(0)
     k0, k1, kc, g0, g1, g2, g3, gc = lax.fori_loop(0, nodes, search, (zero,) * 8)
+    depth = depths[me]
     near_core = core == 0
     picks = [jnp.where(near_core, k0, g0), jnp.where(near_core, k1, g1), g2, g3]
     own_count = jnp.where(near_core, kc, gc)
     own_apart = jnp.where(near_core, 1, 2)
 
-    pl.semaphore_wait(barrier, nodes)
-
-    def pick(held, node, wanted):
-        rows = held[node]
-        return jnp.where(wanted, rows, jnp.zeros_like(rows))
-
-    def send(step, held, solved):
-        held[me] = solved.astype(jnp.bfloat16)
-
-        def start(offset, carry):
-            peer = lax.rem(me + offset, nodes)
-            pltpu.make_async_remote_copy(
-                src_ref=held.at[me], dst_ref=held.at[me],
-                send_sem=send_sem.at[step], recv_sem=recv_sem.at[step],
-                device_id=(peer, core), device_id_type=MESH).start()
-            return carry
-
-        lax.fori_loop(1, nodes, start, 0)
-
-    def gather(step, held):
+    def remote(src, dst, send_sem, recv_sem, peer):
+        return pltpu.make_async_remote_copy(
+            src_ref=src, dst_ref=dst, send_sem=send_sem, recv_sem=recv_sem,
+            device_id=(peer, core), device_id_type=MESH)
+
+    def send(step, slot_list, solved):
+        if step == 0:
+            pl.semaphore_wait(barrier, len(peers) + 1)
         level = levels - 1 - step
-        everyone = held.at[pl.ds(0, nodes - 1)]
-        pltpu.make_async_copy(everyone, everyone, recv_sem.at[step]).wait()
+        planes = slot_list[0]
+        column = slot_list[1] if len(slot_list) > 1 else planes.at[my_spot]
+        column[my_line] = solved.astype(jnp.bfloat16)
+        mine = column.at[my_line]
+        for o in range(1, lines):
+            remote(mine, mine, line_send.at[step], line_recv.at[step, o - 1], along(o)).start()
+
+        def spread(ref):
+            for o in range(1, inner):
+                remote(ref, ref, plane_send.at[step], plane_recv.at[step], within(o)).start()
+
+        def landed(o):
+            from_line = column.at[lax.rem(my_line + lines - o, lines)]
+            pltpu.make_async_copy(from_line, from_line, line_recv.at[step, o - 1]).wait()
+            return from_line
+
+        if len(slot_list) == 1:
+            spread(mine)
+            for o in range(1, lines):
+                spread(landed(o))
+        else:
+            keep = planes.shape[1]
+            chosen = [zero] * keep
+            count = zero
+            for q in range(lines):
+                here = depths[q * inner + my_spot] == level
+                chosen = [jnp.where(here & (count == j), q, chosen[j]) for j in range(keep)]
+                count = count + here.astype(jnp.int32)
+            for o in range(1, lines):
+                landed(o)
+            for j in range(keep):
+                planes[my_spot, j] = column[chosen[j]]
+            spread(planes.at[my_spot])
+
+    def gather(step, slot_list):
+        level = levels - 1 - step
+        planes = slot_list[0]
+
+        def pick(node, wanted):
+            line = lax.div(node, inner)
+            spot = lax.rem(node, inner)
+            if len(slot_list) > 1:
+                place = zero
+                for q in range(lines):
+                    here = (depths[q * inner + spot] == level) & (q < line)
+                    place = place + here.astype(jnp.int32)
+                place = jnp.minimum(place, planes.shape[1] - 1)
+            else:
+                place = line
+            rows = planes[spot, place]
+            return jnp.where(wanted, rows, jnp.zeros_like(rows))
+
+        everyone = planes.at[pl.ds(0, inner - 1)]
+        pltpu.make_async_copy(everyone, everyone, plane_recv.at[step]).wait()
         is_kid = depth + 1 == level
-        kid_a = pick(held, k0, is_kid & (kc > 0))
-        kid_b = pick(held, k1, is_kid & (kc > 1))
+        kid_a = pick(k0, is_kid & (kc > 0))
+        kid_b = pick(k1, is_kid & (kc > 1))
         kids_out[step, :, :width] = kid_a
         kids_out[step, :, width:] = kid_b
         rows_copy = pltpu.make_async_remote_copy(
@@ -129,10 +176,7 @@
             device_id=(me, 1 - core), device_id_type=MESH)
         rows_copy.start()
         mine = depth + own_apart == level
-        four = [pick(held, picks[0], mine & (own_count > 0)),
-                pick(held, picks[1], mine & (own_count > 1)),
-                pick(held, picks[2], mine & (own_count > 2)),
-                pick(held, picks[3], mine & (own_count > 3))]
+        four = [pick(picks[j], mine & (own_count > j)) for j in range(4)]
         four = jnp.concatenate(four, 1)
         own = lax.dot_general(four, four, (((1,), (1,)), ((), ())),
                               preferred_element_type=jnp.float32)
@@ -149,7 +193,16 @@
         acc[:, width:] = acc[:, width:] - jnp.where(near_core, cross, 0.0)
         part_copy.wait()
         acc[:, :width] = acc[:, :width] - (own + got_part[step])
-        pltpu.make_async_copy(everyone, everyone, send_sem.at[step]).wait()
+        pltpu.make_async_copy(everyone, everyone, plane_send.at[step]).wait()
+        column = slot_list[1] if len(slot_list) > 1 else planes.at[0]
+        others = column.at[pl.ds(0, lines - 1)]
+        pltpu.make_async_copy(others, others, line_send.at[step]).wait()
+
+    slots = list(slots)
+    slot_lists = []
+    for step in range(levels - 1):
+        compact = slots[0].shape[1] < lines
+        slot_lists.append([slots.pop(0) for _ in range(1 + compact)])
 
     def level_step(step, carry):
         level = levels - 1 - step
@@ -159,7 +212,7 @@
         active = depth == level
 
         for turn in range(levels - 1):
-            pl.when(step == turn)(functools.partial(send, turn, slots[turn], solved))
+            pl.when(step == turn)(functools.partial(send, turn, slot_lists[turn], solved))
 
         tri = lax.broadcasted_iota(jnp.int32, (width, width), 0)
         tri = tri >= lax.broadcasted_iota(jnp.int32, (width, width), 1)
@@ -168,7 +221,7 @@
         out_panel[...] = jnp.where(active, solved, out_panel[...])
 
         for turn in range(levels - 1):
-            pl.when(step == turn)(functools.partial(gather, turn, slots[turn]))
+            pl.when(step == turn)(functools.partial(gather, turn, slot_lists[turn]))
 
         return carry
 
@@ -182,23 +235,36 @@
     nodes = targets.shape[0]
     levels = nodes.bit_length()
     steps = levels - 1
+    inner = 1
+    while inner * inner * 4 <= nodes:
+        inner *= 2
+    lines = nodes // inner
+    slots = []
+    for level in range(levels - 1, 0, -1):
+        present = min(2**level, nodes - 2**level + 1)
+        keep = min(lines, present)
+        slots.append(pltpu.VMEM((inner, keep, width, width), jnp.bfloat16))
+        if keep < lines:
+            slots.append(pltpu.VMEM((lines, width, width), jnp.bfloat16))
     vmem = pl.BlockSpec(memory_space=pltpu.VMEM)
     dma = pltpu.SemaphoreType.DMA
     square = jax.ShapeDtypeStruct((width, width), jnp.float32)
     lower, solved = pl.pallas_call(
-        functools.partial(kernel, nodes, levels),
+        functools.partial(kernel, nodes, levels, inner),
         out_shape=(square, square),
         in_specs=[pl.BlockSpec(memory_space=pltpu.SMEM), vmem, vmem],
         out_specs=(vmem, vmem),
         scratch_shapes=[
             pltpu.VMEM((width, 2 * width), jnp.float32),
             pltpu.VMEM((width, 2 * width), jnp.float32),
+            pltpu.SMEM((nodes,), jnp.int32),
             pltpu.VMEM((steps, width, width), jnp.float32),
             pltpu.VMEM((steps, width, width), jnp.float32),
             pltpu.VMEM((steps, width, 2 * width), jnp.bfloat16),
             pltpu.VMEM((steps, width, 2 * width), jnp.bfloat16),
-            dma((steps,)), dma((steps,)), dma((steps, 2)), dma((steps, 2)),
-        ] + [pltpu.VMEM((nodes, width, width), jnp.bfloat16)] * steps,
+            dma((steps,)), dma((steps, lines - 1)), dma((steps,)), dma((steps,)),
+            dma((steps, 2)), dma((steps, 2)),
+        ] + slots,
         compiler_params=pltpu.CompilerParams(collective_id=0, has_side_effects=True),
     )(targets, diag_blocks.reshape(width, width), panel_blocks.reshape(width, width))
     return lower[None], solved[None, None]

time: 90 us -> 73.7 us (0.82)
  the two profiles are of different devices: /device:TPU:13 before, /device:TPU:1 now
where the time goes in v2:
time: 73.7 us; the launch traced here: 73.3 us
  Pallas kernels  69.2 us (94%)
  local copies, waits for them, and re-layouts  3.49 us (5%)
    pallas_call x1, Pallas kernels, shards(): pl.pallas_call(functools.partial(kernel, nodes, levels, inner), out_shape...  69.2 us
    unnamed x7, local copies, waits for them, and re-layouts  3.49 us

profile of v2, /device:TPU:1, one launch (start us, length us, event | category | flops | bytes accessed | tf_op | source)
XLA Modules:
  0.0 73.3 jit_solution(16191696146064816844)
XLA Ops:
  0.6 0.0 copy-start.1
  0.6 0.7 copy-done.1
  1.3 0.7 copy.5.targets
  2.0 69.2 %shard_map.50 = (f32[128,128]{1,0:T(8,128)}, f32[128,128]{1,0:T(8,128)}) custom-call(s32[16,2]{1,0:T(8,128)} %copy.5.targets, f32[128,128]{1,0:T(8,128)} %bitcast.4, f32[128,128]{1,0:T(8,128)} %bitcast.5), custom_call_target="tpu_custom_call" | custom-call | tf_op jit(solution)/shard_map/pallas_call | solution.py:252
  71.2 0.0 copy-start
  71.2 1.5 %copy.8 = f32[1,128,128]{2,1,0:T(8,128)} copy(f32[1,128,128]{2,1,0:T(8,128)} %bitcast.7) | data formatting | bytes 131072
  72.7 0.0 copy-done
  72.7 0.6 copy.9
Async XLA Ops:
  0.6 0.7 copy-start.1
  71.2 1.5 %copy-start = (f32[128,128]{1,0:T(8,128)S(1)}, f32[128,128]{1,0:T(8,128)}, u32[]{:S(2)}) copy-start(f32[128,128]{1,0:T(8,128)} %get-tuple-element.5) | copy-start | bytes 196612

commit v3 on v2

--- a/solution.py
+++ b/solution.py
@@ -9,6 +9,7 @@
 
 MESH = pl.DeviceIdType.MESH
 BLOCK = 16
+HALVES = 2
 HIGHEST = lax.Precision.HIGHEST
 
 
@@ -16,9 +17,9 @@
     return jnp.broadcast_to(value, (value.shape[0], width))
 
 
-def factor_rows(work, width):
+def factor_rows(work, width, start, stop):
     total = 2 * width
-    for first in range(0, width, BLOCK):
+    for first in range(start, stop, BLOCK):
         rows = work[first:first + BLOCK, :]
         columns = [across(rows[:, first + j:first + j + 1], 128) for j in range(BLOCK)]
         index = lax.broadcasted_iota(jnp.int32, (BLOCK, 128), 0)
@@ -50,6 +51,7 @@
            got_part, kids_out, kids_in, line_send, line_recv, plane_send, plane_recv, pair_send,
            pair_recv, *slots):
     width = diag.shape[-1]
+    depth_rows = width // HALVES
     lines = nodes // inner
     me = lax.axis_index("col")
     core = lax.axis_index("grp")
@@ -107,30 +109,42 @@
             src_ref=src, dst_ref=dst, send_sem=send_sem, recv_sem=recv_sem,
             device_id=(peer, core), device_id_type=MESH)
 
-    def send(step, slot_list, solved):
-        if step == 0:
+    def column_of(slot_list):
+        return slot_list[1] if len(slot_list) > 1 else slot_list[0].at[my_spot]
+
+    def rows_of(half):
+        return pl.ds(half * depth_rows, depth_rows)
+
+    def spread(step, half, ref):
+        for o in range(1, inner):
+            remote(ref, ref, plane_send.at[step], plane_recv.at[step], within(o)).start()
+
+    def send(step, slot_list, half):
+        if step == 0 and half == 0:
             pl.semaphore_wait(barrier, len(peers) + 1)
+        column = column_of(slot_list)
+        mine = column.at[my_line, rows_of(half)]
+        mine[...] = work[rows_of(half), width:].astype(jnp.bfloat16)
+        for o in range(1, lines):
+            remote(mine, mine, line_send.at[step], line_recv.at[step, half, o - 1],
+                   along(o)).start()
+        if len(slot_list) == 1:
+            spread(step, half, mine)
+
+    def relay(step, slot_list):
         level = levels - 1 - step
         planes = slot_list[0]
-        column = slot_list[1] if len(slot_list) > 1 else planes.at[my_spot]
-        column[my_line] = solved.astype(jnp.bfloat16)
-        mine = column.at[my_line]
-        for o in range(1, lines):
-            remote(mine, mine, line_send.at[step], line_recv.at[step, o - 1], along(o)).start()
-
-        def spread(ref):
-            for o in range(1, inner):
-                remote(ref, ref, plane_send.at[step], plane_recv.at[step], within(o)).start()
-
-        def landed(o):
-            from_line = column.at[lax.rem(my_line + lines - o, lines)]
-            pltpu.make_async_copy(from_line, from_line, line_recv.at[step, o - 1]).wait()
+        column = column_of(slot_list)
+
+        def landed(half, o):
+            from_line = column.at[lax.rem(my_line + lines - o, lines), rows_of(half)]
+            pltpu.make_async_copy(from_line, from_line, line_recv.at[step, half, o - 1]).wait()
             return from_line
 
         if len(slot_list) == 1:
-            spread(mine)
-            for o in range(1, lines):
-                spread(landed(o))
+            for half in range(HALVES):
+                for o in range(1, lines):
+                    spread(step, half, landed(half, o))
         else:
             keep = planes.shape[1]
             chosen = [zero] * keep
@@ -139,11 +153,12 @@
                 here = depths[q * inner + my_spot] == level
                 chosen = [jnp.where(here & (count == j), q, chosen[j]) for j in range(keep)]
                 count = count + here.astype(jnp.int32)
-            for o in range(1, lines):
-                landed(o)
+            for half in range(HALVES):
+                for o in range(1, lines):
+                    landed(half, o)
             for j in range(keep):
                 planes[my_spot, j] = column[chosen[j]]
-            spread(planes.at[my_spot])
+            spread(step, 0, planes.at[my_spot])
 
     def gather(step, slot_list):
         level = levels - 1 - step
@@ -168,17 +183,17 @@
         is_kid = depth + 1 == level
         kid_a = pick(k0, is_kid & (kc > 0))
         kid_b = pick(k1, is_kid & (kc > 1))
-        kids_out[step, :, :width] = kid_a
-        kids_out[step, :, width:] = kid_b
+        kids_out[step, :width] = kid_a
+        kids_out[step, width:] = kid_b
         rows_copy = pltpu.make_async_remote_copy(
             src_ref=kids_out.at[step], dst_ref=kids_in.at[step],
             send_sem=pair_send.at[step, 0], recv_sem=pair_recv.at[step, 0],
             device_id=(me, 1 - core), device_id_type=MESH)
-        rows_copy.start()
+        pl.when(core == 1)(rows_copy.start)
         mine = depth + own_apart == level
         four = [pick(picks[j], mine & (own_count > j)) for j in range(4)]
-        four = jnp.concatenate(four, 1)
-        own = lax.dot_general(four, four, (((1,), (1,)), ((), ())),
+        four = jnp.concatenate(four, 0)
+        own = lax.dot_general(four, four, (((0,), (0,)), ((), ())),
                               preferred_element_type=jnp.float32)
         part[step] = own
         part_copy = pltpu.make_async_remote_copy(
@@ -186,17 +201,31 @@
             send_sem=pair_send.at[step, 1], recv_sem=pair_recv.at[step, 1],
             device_id=(me, 1 - core), device_id_type=MESH)
         part_copy.start()
-        rows_copy.wait()
-        kids = jnp.concatenate([kid_a, kid_b], 1)
-        cross = lax.dot_general(kids, kids_in[step], (((1,), (1,)), ((), ())),
-                                preferred_element_type=jnp.float32)
-        acc[:, width:] = acc[:, width:] - jnp.where(near_core, cross, 0.0)
-        part_copy.wait()
+
+        @pl.when(core == 0)
+        def _():
+            rows_copy.wait_recv()
+            kids = jnp.concatenate([kid_a, kid_b], 0)
+            cross = lax.dot_general(kids, kids_in[step], (((0,), (0,)), ((), ())),
+                                    preferred_element_type=jnp.float32)
+            acc[:, width:] = acc[:, width:] - cross
+
+        part_copy.wait_recv()
         acc[:, :width] = acc[:, :width] - (own + got_part[step])
+
+    def settle(step, slot_list):
+        planes = slot_list[0]
+        everyone = planes.at[pl.ds(0, inner - 1)]
         pltpu.make_async_copy(everyone, everyone, plane_send.at[step]).wait()
-        column = slot_list[1] if len(slot_list) > 1 else planes.at[0]
-        others = column.at[pl.ds(0, lines - 1)]
+        others = column_of(slot_list).at[pl.ds(0, lines - 1)]
         pltpu.make_async_copy(others, others, line_send.at[step]).wait()
+        sent = part.at[step]
+        pltpu.make_async_copy(sent, sent, pair_send.at[step, 1]).wait()
+
+        @pl.when(core == 1)
+        def _():
+            kids = kids_out.at[step]
+            pltpu.make_async_copy(kids, kids, pair_send.at[step, 0]).wait()
 
     slots = list(slots)
     slot_lists = []
@@ -207,18 +236,20 @@
     def level_step(step, carry):
         level = levels - 1 - step
         work[...] = acc[...]
-        factor_rows(work, width)
-        solved = work[:, width:].T
         active = depth == level
+        for half in range(HALVES):
+            factor_rows(work, width, half * depth_rows, (half + 1) * depth_rows)
+            for turn in range(levels - 1):
+                pl.when(step == turn)(functools.partial(send, turn, slot_lists[turn], half))
 
         for turn in range(levels - 1):
-            pl.when(step == turn)(functools.partial(send, turn, slot_lists[turn], solved))
+            pl.when(step == turn)(functools.partial(relay, turn, slot_lists[turn]))
 
         tri = lax.broadcasted_iota(jnp.int32, (width, width), 0)
         tri = tri >= lax.broadcasted_iota(jnp.int32, (width, width), 1)
         lower = jnp.where(tri, work[:, :width].T, 0.0)
         out_diag[...] = jnp.where(active, lower, out_diag[...])
-        out_panel[...] = jnp.where(active, solved, out_panel[...])
+        out_panel[...] = jnp.where(active, work[:, width:].T, out_panel[...])
 
         for turn in range(levels - 1):
             pl.when(step == turn)(functools.partial(gather, turn, slot_lists[turn]))
@@ -228,6 +259,8 @@
     out_diag[...] = jnp.zeros_like(out_diag)
     out_panel[...] = jnp.zeros_like(out_panel)
     lax.fori_loop(0, levels, level_step, 0)
+    for turn in range(levels - 1):
+        settle(turn, slot_lists[turn])
 
 
 def shards(diag_blocks, panel_blocks, targets):
@@ -260,9 +293,9 @@
             pltpu.SMEM((nodes,), jnp.int32),
             pltpu.VMEM((steps, width, width), jnp.float32),
             pltpu.VMEM((steps, width, width), jnp.float32),
-            pltpu.VMEM((steps, width, 2 * width), jnp.bfloat16),
-            pltpu.VMEM((steps, width, 2 * width), jnp.bfloat16),
-            dma((steps,)), dma((steps, lines - 1)), dma((steps,)), dma((steps,)),
+            pltpu.VMEM((steps, 2 * width, width), jnp.bfloat16),
+            pltpu.VMEM((steps, 2 * width, width), jnp.bfloat16),
+            dma((steps,)), dma((steps, HALVES, lines - 1)), dma((steps,)), dma((steps,)),
             dma((steps, 2)), dma((steps, 2)),
         ] + slots,
         compiler_params=pltpu.CompilerParams(collective_id=0, has_side_effects=True),

time: 73.7 us -> 67.9 us (0.921)
  Pallas kernels: 69.2 us -> 63.5 us
    pallas_call x1, Pallas kernels: 69.2 us -> 63.5 us  [shards(): pl.pallas_call(functools.partial(kernel, nodes, levels, inner), out_shape...]
where the time goes in v3:
time: 67.9 us; the launch traced here: 67.7 us
  Pallas kernels  63.5 us (94%)
  local copies, waits for them, and re-layouts  3.49 us (5%)
    pallas_call x1, Pallas kernels, shards(): pl.pallas_call(functools.partial(kernel, nodes, levels, inner), out_shape...  63.5 us
    unnamed x7, local copies, waits for them, and re-layouts  3.49 us

profile of v3, /device:TPU:1, one launch (start us, length us, event | category | flops | bytes accessed | tf_op | source)
XLA Modules:
  0.0 67.7 jit_solution(4569407051830916234)
XLA Ops:
  0.6 0.0 copy-start.1
  0.6 0.7 copy-done.1
  1.3 0.7 %copy.5.targets = s32[16,2]{1,0:T(8,128)} copy(s32[16,2]{0,1:T(2,128)S(1)} %copy-done.1) | data formatting | bytes 256 | tf_op args[2]
  2.0 63.5 %shard_map.50 = (f32[128,128]{1,0:T(8,128)}, f32[128,128]{1,0:T(8,128)}) custom-call(s32[16,2]{1,0:T(8,128)} %copy.5.targets, f32[128,128]{1,0:T(8,128)} %bitcast.4, f32[128,128]{1,0:T(8,128)} %bitcast.5), custom_call_target="tpu_custom_call" | custom-call | tf_op jit(solution)/shard_map/pallas_call | solution.py:285
  65.5 0.0 copy-start
  65.5 1.5 %copy.8 = f32[1,128,128]{2,1,0:T(8,128)} copy(f32[1,128,128]{2,1,0:T(8,128)} %bitcast.7) | data formatting | bytes 131072
  67.0 0.0 copy-done
  67.0 0.6 copy.9
Async XLA Ops:
  0.6 0.7 %copy-start.1 = (s32[16,2]{0,1:T(2,128)S(1)}, s32[16,2]{0,1:T(2,128)}, u32[]{:S(2)}) copy-start(s32[16,2]{0,1:T(2,128)} %param.5) | copy-start | bytes 388
  65.5 1.5 %copy-start = (f32[128,128]{1,0:T(8,128)S(1)}, f32[128,128]{1,0:T(8,128)}, u32[]{:S(2)}) copy-start(f32[128,128]{1,0:T(8,128)} %get-tuple-element.5) | copy-start | bytes 196612

commit v4 on v3

--- a/solution.py
+++ b/solution.py
@@ -74,12 +74,12 @@
     acc[:, width:] = panel[...].T
 
     def parent_of(node):
-        return jnp.where(node < nodes, targets[jnp.minimum(node, nodes - 1), 0], nodes)
+        return jnp.where(node < nodes, targets[0, jnp.minimum(node, nodes - 1)], nodes)
 
     def search(node, carry):
-        current = targets[node, 0]
+        current = targets[0, node]
         kid = current == me
-        grand = targets[node, 1] == me
+        grand = targets[1, node] == me
         level = jnp.int32(0)
         for _ in range(levels - 1):
             level = level + (current < nodes).astype(jnp.int32)
@@ -281,7 +281,7 @@
             slots.append(pltpu.VMEM((lines, width, width), jnp.bfloat16))
     vmem = pl.BlockSpec(memory_space=pltpu.VMEM)
     dma = pltpu.SemaphoreType.DMA
-    square = jax.ShapeDtypeStruct((width, width), jnp.float32)
+    square = pltpu.VMEM((width, width), jnp.float32)
     lower, solved = pl.pallas_call(
         functools.partial(kernel, nodes, levels, inner),
         out_shape=(square, square),
@@ -299,7 +299,7 @@
             dma((steps, 2)), dma((steps, 2)),
         ] + slots,
         compiler_params=pltpu.CompilerParams(collective_id=0, has_side_effects=True),
-    )(targets, diag_blocks.reshape(width, width), panel_blocks.reshape(width, width))
+    )(targets.T, diag_blocks.reshape(width, width), panel_blocks.reshape(width, width))
     return lower[None], solved[None, None]
 
 

time: 67.9 us -> 64.9 us (0.956)
  local copies, waits for them, and re-layouts: 3.49 us -> 1.26 us
  Pallas kernels: 63.5 us -> 62.8 us
    unnamed x7 -> x2, local copies, waits for them, and re-layouts: 3.49 us -> 1.26 us
    pallas_call x1, Pallas kernels: 63.5 us -> 62.8 us  [shards(): pl.pallas_call(functools.partial(kernel, nodes, levels, inner), out_shape...]
where the time goes in v4:
time: 64.9 us; the launch traced here: 64.7 us
  Pallas kernels  62.8 us (97%)
  local copies, waits for them, and re-layouts  1.26 us (2%)
    pallas_call x1, Pallas kernels, shards(): pl.pallas_call(functools.partial(kernel, nodes, levels, inner), out_shape...  62.8 us

profile of v4, /device:TPU:1, one launch (start us, length us, event | category | flops | bytes accessed | tf_op | source)
XLA Modules:
  0.0 64.7 jit_solution(4125987322823454169)
XLA Ops:
  0.6 62.8 %shard_map.50 = (f32[128,128]{1,0:T(8,128)S(1)}, f32[128,128]{1,0:T(8,128)S(1)}) custom-call(s32[2,16]{1,0:T(2,128)} %bitcast.9, f32[128,128]{1,0:T(8,128)} %bitcast.7, f32[128,128]{1,0:T(8,128)} %bitcast.8), custom_call_target="tpu_custom_call" | custom-call | tf_op jit(solution)/shard_map/pallas_call | solution.py:285
  63.5 0.6 copy.7
  64.1 0.6 copy.8

commit v5 on v4

--- a/solution.py
+++ b/solution.py
@@ -8,7 +8,7 @@
 from jax.sharding import PartitionSpec as P
 
 MESH = pl.DeviceIdType.MESH
-BLOCK = 16
+BLOCK = 32
 HALVES = 2
 HIGHEST = lax.Precision.HIGHEST
 
@@ -41,9 +41,15 @@
         upper = jnp.concatenate(done, 0)
         work[first:first + BLOCK, :] = upper
         if first + BLOCK < width:
-            left = upper[:, :width]
-            change = lax.dot_general(left, upper, (((0,), (0,)), ((), ())),
-                                     precision=HIGHEST, preferred_element_type=jnp.float32)
+            high = upper.astype(jnp.bfloat16)
+            rest = upper - high.astype(jnp.float32)
+            middle = rest.astype(jnp.bfloat16)
+            low = (rest - middle.astype(jnp.float32)).astype(jnp.bfloat16)
+            left = [term[:, :width] for term in (high, high, high, middle, middle, low)]
+            left = jnp.concatenate(left, 0)
+            right = jnp.concatenate([high, middle, low, high, middle, high], 0)
+            change = lax.dot_general(left, right, (((0,), (0,)), ((), ())),
+                                     preferred_element_type=jnp.float32)
             work[first + BLOCK:, :] = work[first + BLOCK:, :] - change[first + BLOCK:, :]
 
 

time: 64.9 us -> 58.8 us (0.906)
  Pallas kernels: 62.8 us -> 56.7 us
    pallas_call x1, Pallas kernels: 62.8 us -> 56.7 us  [shards(): pl.pallas_call(functools.partial(kernel, nodes, levels, inner), out_shape...]
where the time goes in v5:
time: 58.8 us; the launch traced here: 58.6 us
  Pallas kernels  56.7 us (96%)
  local copies, waits for them, and re-layouts  1.26 us (2%)
  between operations  0.64 us (1%)
    pallas_call x1, Pallas kernels, shards(): pl.pallas_call(functools.partial(kernel, nodes, levels, inner), out_shape...  56.7 us
    unnamed x2, local copies, waits for them, and re-layouts  1.26 us

profile of v5, /device:TPU:1, one launch (start us, length us, event | category | flops | bytes accessed | tf_op | source)
XLA Modules:
  0.0 58.6 jit_solution(16561511803016550055)
XLA Ops:
  0.6 56.7 %shard_map.50 = (f32[128,128]{1,0:T(8,128)S(1)}, f32[128,128]{1,0:T(8,128)S(1)}) custom-call(s32[2,16]{1,0:T(2,128)} %bitcast.9, f32[128,128]{1,0:T(8,128)} %bitcast.7, f32[128,128]{1,0:T(8,128)} %bitcast.8), custom_call_target="tpu_custom_call" | custom-call | tf_op jit(solution)/shard_map/pallas_call | solution.py:291
  57.3 0.6 %copy.7 = f32[1,128,128]{2,1,0:T(8,128)} copy(f32[1,128,128]{2,1,0:T(8,128)S(1)} %bitcast.6) | data formatting | bytes 131072
  58.0 0.6 %copy.8 = f32[1,1,128,128]{3,2,1,0:T(8,128)} copy(f32[1,1,128,128]{3,2,1,0:T(8,128)S(1)} %bitcast.5) | data formatting | bytes 131072
